TPU v7x, 256 devices: a whole 4x4x8 slice. The times are simulated.
256 devices in a mesh: replica: 16 (over z, core), mp: 16 (over y, x).
Axes of the slice: x: 4, y: 4, z: 8, core: 2. Of those that a mesh axis runs over, the one named last changes fastest.
Arguments:
- gradients: bfloat16 [16, 8, 768, 3072], P('replica', None, 'mp'), may hold values from -6 to 6
- feedback: bfloat16 [16, 8, 768, 3072], P('replica', None, 'mp'), may hold values from -4 to 4
- right_init: bfloat16 [8, 3072, 32], replicated, may hold values from -0.109375 to 0.109375
- gram_root: float32 [8, 32, 32], replicated, as said below
- owners: int32 [8], replicated, may hold values from 0 to 15, as said below
- momentum: float32 [16, 1, 768, 3072], P('mp', None, 'replica'), may hold values from -4 to 4
- master_weights: float32 [16, 1, 768, 3072], P('mp', None, 'replica'), may hold values from -1.5 to 1.5
- vector_grads: float32 [16, 10752], P('replica', 'mp'), may hold values from -6 to 6
- vector_momentum: float32 [10752], P('mp'), may hold values from -6 to 6
- vector_params: float32 [10752], P('mp'), may hold values from -6 to 6
Outputs:
- new_feedback: bfloat16 [16, 8, 768, 3072], P('replica', None, 'mp')
- new_momentum: float32 [16, 1, 768, 3072], P('mp', None, 'replica')
- new_master: float32 [16, 1, 768, 3072], P('mp', None, 'replica')
- new_weights: bfloat16 [8, 768, 3072], P(None, 'replica')
- new_vector_momentum: float32 [10752], P('mp')
- new_vector_params: float32 [10752], P('mp')
Inputs may be any that keep to these rules, and one draw needn't show every extreme that they name: `owners`: every matrix has one owner; no owner holds more than 1 of the 8 matrices, and one owner holds exactly 1. `gram_root`: each matrix is the identity plus off-diagonal terms, times a positive scale.
All inputs are finite; a program needn't handle non-finite values.
Results may differ from a plain program's by a relative error of at most 0.007.
Values may be sent and summed in bfloat16 or wider, within the bound.
A program may use at most 192 MiB of HBM per device.

v0:
```python
import jax
import jax.numpy as jnp
from jax import lax
from jax.sharding import PartitionSpec as P


def per_device(
    gradients,
    feedback,
    right_init,
    gram_root,
    owners,
    momentum,
    master_weights,
    vector_grads,
    vector_momentum,
    vector_params,
):
    highest = lax.Precision.HIGHEST
    compensated = (gradients[0].astype(jnp.float32) + feedback[0].astype(jnp.float32)).astype(
        jnp.bfloat16
    )
    owner_count = lax.axis_size("mp")
    capacity = momentum.shape[1]
    matrices = owners.shape[0]
    replica_rows = momentum.shape[2]
    mp_index = lax.axis_index("mp")
    replica_index = lax.axis_index("replica")
    same_owner = owners[:, None] == owners[None, :]
    earlier = jnp.arange(matrices)[:, None] < jnp.arange(matrices)[None, :]
    ranks = jnp.sum((same_owner & earlier).astype(jnp.int32), axis=0)
    slots = owners * capacity + ranks
    mine = slots[None, :] == (mp_index * capacity + jnp.arange(capacity))[:, None]
    has = jnp.any(mine, axis=1)
    chosen = jnp.argmax(mine, axis=1)
    left_terms = jnp.einsum(
        "kmn,knr->kmr", compensated, right_init, preferred_element_type=jnp.float32
    )
    left_sum = lax.psum(left_terms, "replica")
    left_rows = jnp.einsum("kmr,krs->kms", left_sum, gram_root, precision=highest).astype(
        jnp.bfloat16
    )
    right_terms = jnp.einsum(
        "kmn,kms->kns", compensated, left_rows, preferred_element_type=jnp.float32
    )
    right_part = lax.psum_scatter(right_terms.reshape(-1), "mp", scatter_dimension=0, tiled=True)
    right_part = lax.psum(right_part, "replica")
    right_new = lax.all_gather(right_part.astype(jnp.bfloat16), "mp", axis=0, tiled=True).reshape(
        right_terms.shape
    )
    left_all = lax.all_gather(left_rows, "mp", axis=1, tiled=True)
    approx_rows = jnp.einsum(
        "kms,kns->kmn", left_rows, right_new, preferred_element_type=jnp.float32
    )
    new_feedback = (compensated.astype(jnp.float32) - approx_rows).astype(jnp.bfloat16)
    scale = has.astype(jnp.float32)[:, None, None]
    left_chosen = (
        lax.dynamic_slice_in_dim(
            left_all[chosen], replica_index * replica_rows, replica_rows, 1
        ).astype(jnp.float32)
        * scale
    )
    right_chosen = right_new[chosen].astype(jnp.float32) * scale
    approx_slots = jnp.einsum("cmr,cnr->cmn", left_chosen, right_chosen, precision=highest)
    new_momentum = 0.9 * momentum[0] + approx_slots
    new_master = master_weights[0] - 0.1 * new_momentum
    master_narrow = new_master.astype(jnp.bfloat16)
    weight_slots = lax.all_gather(master_narrow, "mp", axis=0, tiled=True)
    new_weights = jnp.take(weight_slots, slots, axis=0)
    vector_total = lax.psum(vector_grads[0], "replica")
    new_vector_momentum = 0.9 * vector_momentum + vector_total
    new_vector_params = vector_params - 0.1 * new_vector_momentum
    return (
        new_feedback[None],
        new_momentum[None],
        new_master[None],
        new_weights,
        new_vector_momentum,
        new_vector_params,
    )


def solution(mesh):
    return jax.shard_map(
        per_device,
        mesh=mesh,
        in_specs=(
            P("replica", None, "mp", None),
            P("replica", None, "mp", None),
            P(),
            P(),
            P(),
            P("mp", None, "replica", None),
            P("mp", None, "replica", None),
            P("replica", "mp"),
            P("mp"),
            P("mp"),
        ),
        out_specs=(
            P("replica", None, "mp", None),
            P("mp", None, "replica", None),
            P("mp", None, "replica", None),
            P(None, "replica", None),
            P("mp"),
            P("mp"),
        ),
        check_vma=False,
    )
```

profile of v0, /device:TPU:1, one launch (start us, length us, event | category | flops | bytes accessed | tf_op | source)
XLA Modules:
  0.0 369.8 jit_solution(15668243150370292519)
XLA Ops:
  7.2 0.0 copy-start
  7.2 0.0 copy-start.4
  7.2 0.0 all-reduce.5.cloned.1.call-start
  7.2 1.3 copy-done
  8.6 3.1 fusion.14
  11.7 49.7 %psum.21 = f32[8,48,32]{1,2,0:T(8,128)S(1)} all-reduce(f32[8,48,32]{1,2,0:T(8,128)S(1)} %fusion.14), channel_id=1, replica_groups=mesh['replica'=16,'mp'=16] {'replica'}, use_global_device_ids=true, to_apply=%region_0.0 | all-reduce | flops 12288 | bytes 98304 | tf_op jit(solution)/shard_map/psum | solution.py:39
  61.4 0.0 copy-done.4
  61.4 0.4 convolution_convert_fusion
  61.8 9.0 %fusion.12 = f32[8,3072,32]{2,1,0:T(8,128)} fusion(bf16[8,48,32]{1,2,0:T(8,128)(2,1)S(1)} %convolution_convert_fusion, bf16[1,8,48,3072]{3,2,1,0:T(8,128)(2,1)} %param.11, bf16[1,8,48,3072]{3,2,1,0:T(8,128)(2,1)} %param.10), kind=kOutput, calls=%fused_computation.29 | convolution fusion | flops 80216064 | bytes 7888896 | tf_op jit(solution)/shard_map/kmn,kms->kns/dot_general | solution.py:43
  70.8 9.4 %reshape.76 = f32[786432]{0:T(1024)} reshape(f32[8,3072,32]{2,1,0:T(8,128)} %fusion.12) | data formatting | bytes 6291456 | tf_op jit(solution)/shard_map/reshape | solution.py:46
  80.2 0.0 copy-start.9
  80.2 0.0 copy-start.7
  80.2 0.0 copy-start.8
  80.2 0.0 all-reduce.5.cloned.1.call-update
  80.2 0.0 all-gather.4.cloned.1.call-start
  80.3 0.6 copy-done.9
  80.9 0.6 dynamic-slice.8
  82.1 0.0 copy-done.7
  82.1 104.3 %all-reduce.5.cloned.1.call-done = f32[786432]{0:T(1024)} async-done(((f32[786432]{0:T(1024)}), f32[786432]{0:T(1024)}) %all-reduce.5.cloned.1.call-update) | async-done | bytes 3145744
  186.4 0.9 dynamic-slice.9
  187.3 48.4 %all-reduce.6 = (bf16[49152]{0:T(1024)(128)(2,1)}, f32[672]{0:T(1024)S(1)}) all-reduce(f32[49152]{0:T(1024)S(1)} %dynamic-slice.9, f32[672]{0:T(1024)S(1)} %reduce.20), channel_id=1, replica_groups=mesh['replica'=16,'mp'=16] {'replica'}, use_global_device_ids=true, to_apply=%region_2.0 | all-reduce | flops 49824 | bytes 300288 | tf_op jit(solution)/shard_map/psum | solution.py:47
  235.7 0.0 all-gather.4.cloned.1.call-update
  235.7 0.0 all-gather.6.cloned.1.call-start
  235.8 0.1 copy.27
  235.9 0.0 copy-done.8
  235.9 0.1 convert_reduce_fusion
  236.0 0.7 bitcast_reduce_fusion
  238.0 0.6 compare_and_fusion
  239.9 21.6 %all_gather.10 = bf16[8,768,32]{2,0,1:T(8,128)(2,1)S(1)} all-gather(bf16[8,48,32]{2,0,1:T(8,128)(2,1)S(1)} %copy.27), channel_id=1, replica_groups=mesh['replica'=16,'mp'=16] {'mp'}, dimensions={1}, use_global_device_ids=true | all-gather | bytes 417792 | tf_op jit(solution)/shard_map/all_gather | solution.py:51
  261.5 0.0 copy-start.2
  261.5 22.4 %all-gather.4.cloned.1.call-done = bf16[786432]{0:T(1024)(128)(2,1)} async-done(((bf16[49152]{0:T(1024)(128)(2,1)}), bf16[786432]{0:T(1024)(128)(2,1)}) %all-gather.4.cloned.1.call-update) | async-done | bytes 1572880 | tf_op jit(solution)/shard_map/all_gather | solution.py:48
  283.9 7.8 %reshape.77 = bf16[8,3072,32]{2,1,0:T(8,128)(2,1)} reshape(bf16[786432]{0:T(1024)(128)(2,1)} %all-gather.4.cloned.1.call-done) | data formatting | bytes 3145728 | tf_op jit(solution)/shard_map/reshape | solution.py:48
  291.7 0.0 copy-start.3
  291.8 0.0 copy-start.5
  291.8 0.0 copy-done.2
  291.8 3.0 convolution_add_fusion
  294.7 0.0 copy-done.3
  294.8 0.0 copy-start.1
  294.8 1.1 fusion.7
  295.9 0.0 all-gather.6.cloned.1.call-update
  295.9 0.0 copy-done.5
  295.9 0.0 copy-done.6
  295.9 0.6 multiply_subtract_fusion
  296.5 7.9 %fusion = bf16[1,8,48,3072]{3,2,1,0:T(8,128)(2,1)} fusion(bf16[8,48,32]{1,2,0:T(8,128)(2,1)S(1)} %convolution_convert_fusion, bf16[8,3072,32]{2,1,0:T(8,128)(2,1)} %reshape.77, bf16[1,8,48,3072]{3,2,1,0:T(8,128)(2,1)} %param.11, bf16[1,8,48,3072]{3,2,1,0:T(8,128)(2,1)} %param.10), kind=kOutput, calls=%fused_computation.3 | convolution fusion | flops 83755008 | bytes 8675328 | tf_op jit(solution)/shard_map/kms,kns->kmn/dot_general | solution.py:52
  304.4 0.0 copy-done.1
  304.4 51.0 %all-gather.6.cloned.1.call-done = bf16[768,3072]{1,0:T(8,128)(2,1)} async-done(((bf16[48,3072]{1,0:T(8,128)(2,1)}), bf16[768,3072]{1,0:T(8,128)(2,1)}) %all-gather.6.cloned.1.call-update) | async-done | bytes 4718608 | tf_op jit(solution)/shard_map/all_gather | solution.py:68
  355.4 4.4 %gather_fusion = bf16[8,48,3072]{2,1,0:T(8,128)(2,1)} fusion(bf16[16,48,3072]{2,1,0:T(8,128)(2,1)} %bitcast.36, s32[1024]{0:T(1024)S(1)} %pad_clamp_fusion), kind=kCustom, calls=%fused_computation | custom fusion | bytes 4718624 | tf_op jit(solution)/shard_map/jit(_take)/gather | solution.py:69
  359.9 3.4 broadcast_select_fusion
  (4 shorter events, 0.1 us)
Async XLA Ops:
  7.2 1.4 copy-start
  7.2 54.2 %copy-start.4 = (f32[8,32,32]{2,1,0:T(8,128)S(1)}, f32[8,32,32]{2,1,0:T(8,128)}, u32[]{:S(2)}) copy-start(f32[8,32,32]{2,1,0:T(8,128)} %param.13) | copy-start | bytes 98308
  7.2 179.2 %all-reduce.5.cloned.1.call-start = ((), (), s32[]{:S(2)}) async-start(), calls=%async_computation.2 | async-start | bytes 6291456
  80.2 0.7 copy-start.9
  80.2 1.9 copy-start.7
  80.2 155.7 %copy-start.8 = (s32[8]{0:T(128)S(1)}, s32[8]{0:T(128)}, u32[]{:S(2)}) copy-start(s32[8]{0:T(128)} %param.14) | copy-start | bytes 100
  80.2 203.7 %all-gather.4.cloned.1.call-start = ((), (), s32[]{:S(2)}) async-start(), calls=%async_computation | async-start | bytes 1671168 | tf_op jit(solution)/shard_map/all_gather | solution.py:48
  235.7 119.7 %all-gather.6.cloned.1.call-start = ((), (), s32[]{:S(2)}) async-start(), calls=%async_computation.1 | async-start | bytes 5013504 | tf_op jit(solution)/shard_map/all_gather | solution.py:68
  261.5 30.2 %copy-start.2 = (f32[1,1,48,3072]{3,2,1,0:T(8,128)S(1)}, f32[1,1,48,3072]{3,2,1,0:T(8,128)}, u32[]{:S(2)}) copy-start(f32[1,1,48,3072]{3,2,1,0:T(8,128)} %param.15) | copy-start | bytes 1769476
  291.7 3.0 copy-start.3
  291.8 4.1 %copy-start.5 = (f32[672]{0:T(1024)S(1)}, f32[672]{0:T(1024)}, u32[]{:S(2)}) copy-start(f32[672]{0:T(1024)} %param.19) | copy-start | bytes 8068
  291.8 4.2 %copy-start.6 = (f32[672]{0:T(1024)S(1)}, f32[672]{0:T(1024)}, u32[]{:S(2)}) copy-start(f32[672]{0:T(1024)} %param.18) | copy-start | bytes 8068
  294.8 9.7 %copy-start.1 = (f32[48,3072]{1,0:T(8,128)}, f32[48,3072]{1,0:T(8,128)S(1)}, u32[]{:S(2)}) copy-start(f32[48,3072]{1,0:T(8,128)S(1)} %convolution_add_fusion) | copy-start | bytes 1769476
Sparse Core Ops, SparseCore 0:
  80.3 106.0 all-reduce.4
  235.8 48.0 all-gather.3
  296.0 59.3 all-gather.5
where the time goes:
time: 370 us
  waiting for transfers between devices  178 us (48%)
  blocking collectives  120 us (32%)
  local copies, waits for them, and re-layouts  25.3 us (7%)
  matrix products  23.4 us (6%)
  between operations  17.2 us (5%)
  other arithmetic  6.49 us (2%)
    unnamed x4, waiting for transfers between devices  104 us
    all_gather x1, waiting for transfers between devices, per_device(): weight_slots = lax.all_gather(master_narrow, 'mp', axis=0, tiled=True)  51 us
    psum x1, blocking collectives, per_device(): left_sum = lax.psum(left_terms, 'replica')  49.7 us
    psum x1, blocking collectives, per_device(): right_part = lax.psum(right_part, 'replica')  48.4 us
    all_gather x1, waiting for transfers between devices, per_device(): lax.all_gather(right_part.astype(jnp.bfloat16), 'mp', axis=0, tiled=True)  22.4 us
    all_gather x1, blocking collectives, per_device(): left_all = lax.all_gather(left_rows, 'mp', axis=1, tiled=True)  21.6 us
    reshape x1, local copies, waits for them, and re-layouts, per_device(): right_terms.reshape(-1)  9.41 us
    dot_general x1, matrix products, per_device(): jnp.einsum('kmn,kms->kns', compensated, left_rows, preferred_element_type...  8.99 us
  transfers between devices with their start and end apart: 3, of which 3 were waited for; matrix products, arithmetic and copies ran while one was open for 3% of the time, Pallas kernels for 0%

commit v1 on v0

--- a/solution.py
+++ b/solution.py
@@ -44,7 +44,8 @@
         "kmn,kms->kns", compensated, left_rows, preferred_element_type=jnp.float32
     )
     right_part = lax.psum_scatter(right_terms.reshape(-1), "mp", scatter_dimension=0, tiled=True)
-    right_part = lax.psum(right_part, "replica")
+    parts = lax.all_gather(right_part, "replica")
+    right_part = jnp.sum(parts, axis=0)
     right_new = lax.all_gather(right_part.astype(jnp.bfloat16), "mp", axis=0, tiled=True).reshape(
         right_terms.shape
     )

time: 370 us -> 370 us (level)
  blocking collectives: 120 us -> 73.1 us
  waiting for transfers between devices: 178 us -> 217 us
  other arithmetic: 6.49 us -> 10.3 us
    psum x1 -> x0, blocking collectives: 48.4 us -> none  [per_device(): right_part = lax.psum(right_part, 'replica')]
    all_gather x0 -> x1, waiting for transfers between devices: none -> 41.7 us  [per_device(): parts = lax.all_gather(right_part, 'replica')]
    unnamed x4 -> x5, waiting for transfers between devices: 104 us -> 104 us
  transfers between devices with their start and end apart: 3 -> 4, of which waited for: 3 -> 4; matrix products, arithmetic and copies ran while one was open for 3% -> 3% of each run, Pallas kernels for 0% -> 0%
where the time goes in v1:
time: 370 us
  waiting for transfers between devices  217 us (59%)
  blocking collectives  73.1 us (20%)
  local copies, waits for them, and re-layouts  28.6 us (8%)
  matrix products  23.4 us (6%)
  between operations  17.2 us (5%)
  other arithmetic  10.3 us (3%)
    unnamed x5, waiting for transfers between devices  104 us
    all_gather x1, waiting for transfers between devices, per_device(): weight_slots = lax.all_gather(master_narrow, 'mp', axis=0, tiled=True)  51 us
    psum x1, blocking collectives, per_device(): left_sum = lax.psum(left_terms, 'replica')  50.5 us
    all_gather x1, waiting for transfers between devices, per_device(): parts = lax.all_gather(right_part, 'replica')  41.7 us
    all_gather x1, blocking collectives, per_device(): left_all = lax.all_gather(left_rows, 'mp', axis=1, tiled=True)  22.6 us
    all_gather x1, waiting for transfers between devices, per_device(): lax.all_gather(right_part.astype(jnp.bfloat16), 'mp', axis=0, tiled=True)  19.9 us
    reshape x1, local copies, waits for them, and re-layouts, per_device(): right_terms.reshape(-1)  9.41 us
    dot_general x1, matrix products, per_device(): jnp.einsum('kmn,kms->kns', compensated, left_rows, preferred_element_type...  8.99 us
  transfers between devices with their start and end apart: 4, of which 4 were waited for; matrix products, arithmetic and copies ran while one was open for 3% of the time, Pallas kernels for 0%

profile of v1, /device:TPU:1, one launch (start us, length us, event | category | flops | bytes accessed | tf_op | source)
XLA Modules:
  0.0 369.6 jit_solution(6850357671872603062)
XLA Ops:
  7.2 0.0 copy-start
  7.2 0.0 all-reduce.4.cloned.1.call-start
  7.2 0.8 reduce.20
  8.0 0.6 copy-done
  8.6 0.0 copy-start.4
  8.6 3.1 fusion.14
  11.7 50.5 %all-reduce.1 = (f32[8,48,32]{1,2,0:T(8,128)S(1)}, f32[672]{0:T(1024)S(1)}) all-reduce(f32[8,48,32]{1,2,0:T(8,128)S(1)} %fusion.14, f32[672]{0:T(1024)S(1)} %reduce.20), channel_id=1, replica_groups=mesh['replica'=16,'mp'=16] {'replica'}, use_global_device_ids=true, to_apply=%region_0.0 | all-reduce | flops 12960 | bytes 103680 | tf_op jit(solution)/shard_map/psum | solution.py:39
  62.2 0.0 copy-done.4
  62.2 0.4 convolution_convert_fusion
  62.6 9.0 %fusion.12 = f32[8,3072,32]{2,1,0:T(8,128)} fusion(bf16[8,48,32]{1,2,0:T(8,128)(2,1)S(1)} %convolution_convert_fusion, bf16[1,8,48,3072]{3,2,1,0:T(8,128)(2,1)} %param.11, bf16[1,8,48,3072]{3,2,1,0:T(8,128)(2,1)} %param.10), kind=kOutput, calls=%fused_computation.29 | convolution fusion | flops 80216064 | bytes 7888896 | tf_op jit(solution)/shard_map/kmn,kms->kns/dot_general | solution.py:43
  71.6 9.4 %reshape.76 = f32[786432]{0:T(1024)} reshape(f32[8,3072,32]{2,1,0:T(8,128)} %fusion.12) | data formatting | bytes 6291456 | tf_op jit(solution)/shard_map/reshape | solution.py:46
  81.0 0.0 copy-start.8
  81.0 0.0 all-reduce.4.cloned.1.call-update
  81.1 0.0 all-gather.8.cloned.1.call-start
  81.1 0.6 copy-done.8
  81.7 0.6 dynamic-slice.8
  83.0 104.2 %all-reduce.4.cloned.1.call-done = f32[786432]{0:T(1024)} async-done(((f32[786432]{0:T(1024)}), f32[786432]{0:T(1024)}) %all-reduce.4.cloned.1.call-update) | async-done | bytes 3145744
  187.1 1.6 dynamic-slice.9
  188.8 0.0 all-gather.8.cloned.1.call-update
  188.8 0.0 all-gather.6.cloned.1.call-start
  188.8 41.7 %all-gather.8.cloned.1.call-done = f32[786432]{0:T(1024)} async-done(((f32[49152]{0:T(1024)}), f32[786432]{0:T(1024)}) %all-gather.8.cloned.1.call-update) | async-done | bytes 3145744 | tf_op jit(solution)/shard_map/all_gather | solution.py:47
  230.5 3.4 reshape.130
  233.9 3.0 reduce_sum.18
  237.0 0.0 all-gather.6.cloned.1.call-update
  237.0 0.0 all-gather.10.cloned.1.call-start
  237.1 0.1 copy.27
  237.2 0.0 copy-done.7
  237.2 0.1 convert_reduce_fusion
  237.3 0.7 bitcast_reduce_fusion
  239.3 0.6 compare_and_fusion
  241.2 22.6 %all_gather.18 = bf16[8,768,32]{2,0,1:T(8,128)(2,1)S(1)} all-gather(bf16[8,48,32]{2,0,1:T(8,128)(2,1)S(1)} %copy.27), channel_id=1, replica_groups=mesh['replica'=16,'mp'=16] {'mp'}, dimensions={1}, use_global_device_ids=true | all-gather | bytes 417792 | tf_op jit(solution)/shard_map/all_gather | solution.py:52
  263.9 0.0 copy-start.2
  263.9 19.9 %all-gather.6.cloned.1.call-done = bf16[786432]{0:T(1024)(128)(2,1)} async-done(((bf16[49152]{0:T(1024)(128)(2,1)}), bf16[786432]{0:T(1024)(128)(2,1)}) %all-gather.6.cloned.1.call-update) | async-done | bytes 1572880 | tf_op jit(solution)/shard_map/all_gather | solution.py:49
  283.8 7.8 %reshape.77 = bf16[8,3072,32]{2,1,0:T(8,128)(2,1)} reshape(bf16[786432]{0:T(1024)(128)(2,1)} %all-gather.6.cloned.1.call-done) | data formatting | bytes 3145728 | tf_op jit(solution)/shard_map/reshape | solution.py:49
  291.6 0.0 copy-done.2
  291.6 3.0 convolution_add_fusion
  294.6 0.0 copy-done.3
  294.6 0.0 copy-start.1
  294.6 1.1 fusion.7
  295.7 0.0 all-gather.10.cloned.1.call-update
  295.8 0.0 copy-done.5
  295.8 0.0 copy-done.6
  295.8 0.6 multiply_subtract_fusion
  296.4 7.9 %fusion = bf16[1,8,48,3072]{3,2,1,0:T(8,128)(2,1)} fusion(bf16[8,48,32]{1,2,0:T(8,128)(2,1)S(1)} %convolution_convert_fusion, bf16[8,3072,32]{2,1,0:T(8,128)(2,1)} %reshape.77, bf16[1,8,48,3072]{3,2,1,0:T(8,128)(2,1)} %param.11, bf16[1,8,48,3072]{3,2,1,0:T(8,128)(2,1)} %param.10), kind=kOutput, calls=%fused_computation.3 | convolution fusion | flops 83755008 | bytes 8675328 | tf_op jit(solution)/shard_map/kms,kns->kmn/dot_general | solution.py:53
  304.3 0.0 copy-done.1
  304.3 51.0 %all-gather.10.cloned.1.call-done = bf16[768,3072]{1,0:T(8,128)(2,1)} async-done(((bf16[48,3072]{1,0:T(8,128)(2,1)}), bf16[768,3072]{1,0:T(8,128)(2,1)}) %all-gather.10.cloned.1.call-update) | async-done | bytes 4718608 | tf_op jit(solution)/shard_map/all_gather | solution.py:69
  355.3 4.4 %gather_fusion = bf16[8,48,3072]{2,1,0:T(8,128)(2,1)} fusion(bf16[16,48,3072]{2,1,0:T(8,128)(2,1)} %bitcast.36, s32[1024]{0:T(1024)S(1)} %pad_clamp_fusion), kind=kCustom, calls=%fused_computation | custom fusion | bytes 4718624 | tf_op jit(solution)/shard_map/jit(_take)/gather | solution.py:70
  359.7 3.4 broadcast_select_fusion
  (6 shorter events, 0.0 us)
Async XLA Ops:
  7.2 1.4 copy-start
  7.2 180.0 %all-reduce.4.cloned.1.call-start = ((), (), s32[]{:S(2)}) async-start(), calls=%async_computation.3 | async-start | bytes 6291456
  8.6 53.6 %copy-start.4 = (f32[8,32,32]{2,1,0:T(8,128)S(1)}, f32[8,32,32]{2,1,0:T(8,128)}, u32[]{:S(2)}) copy-start(f32[8,32,32]{2,1,0:T(8,128)} %param.13) | copy-start | bytes 98308
  81.0 0.7 copy-start.8
  81.1 149.5 %all-gather.8.cloned.1.call-start = ((), (), s32[]{:S(2)}) async-start(), calls=%async_computation.1 | async-start | bytes 3342336 | tf_op jit(solution)/shard_map/all_gather | solution.py:47
  188.8 95.0 %all-gather.6.cloned.1.call-start = ((), (), s32[]{:S(2)}) async-start(), calls=%async_computation | async-start | bytes 1671168 | tf_op jit(solution)/shard_map/all_gather | solution.py:49
  233.9 3.3 copy-start.7
  237.0 118.3 %all-gather.10.cloned.1.call-start = ((), (), s32[]{:S(2)}) async-start(), calls=%async_computation.2 | async-start | bytes 5013504 | tf_op jit(solution)/shard_map/all_gather | solution.py:69
  263.9 27.7 %copy-start.2 = (f32[1,1,48,3072]{3,2,1,0:T(8,128)S(1)}, f32[1,1,48,3072]{3,2,1,0:T(8,128)}, u32[]{:S(2)}) copy-start(f32[1,1,48,3072]{3,2,1,0:T(8,128)} %param.15) | copy-start | bytes 1769476
  291.6 3.0 copy-start.3
  291.6 4.1 %copy-start.5 = (f32[672]{0:T(1024)S(1)}, f32[672]{0:T(1024)}, u32[]{:S(2)}) copy-start(f32[672]{0:T(1024)} %param.19) | copy-start | bytes 8068
  291.6 4.2 %copy-start.6 = (f32[672]{0:T(1024)S(1)}, f32[672]{0:T(1024)}, u32[]{:S(2)}) copy-start(f32[672]{0:T(1024)} %param.18) | copy-start | bytes 8068
  294.6 9.7 %copy-start.1 = (f32[48,3072]{1,0:T(8,128)}, f32[48,3072]{1,0:T(8,128)S(1)}, u32[]{:S(2)}) copy-start(f32[48,3072]{1,0:T(8,128)S(1)} %convolution_add_fusion) | copy-start | bytes 1769476
Sparse Core Ops, SparseCore 0:
  81.2 105.9 all-reduce.3
  189.6 40.9 all-gather.7
  237.1 46.5 all-gather.5
  295.9 59.3 all-gather.9
